TPU v7x, 256 devices: a whole 4x4x8 slice. The times are simulated.
256 devices in a mesh: face: 32 (over z, y_lo, core), depth: 8 (over y_hi, x).
Axes of the slice: x: 4, y: 4 (y_hi: 2, y_lo: 2; y = y_hi * 2 + y_lo), z: 8, core: 2. Of those that a mesh axis runs over, the one named last changes fastest.
Arguments:
- thermal_field: float32 [2, 32, 8, 2048], P(None, 'face', 'depth'), may hold values from -6 to 6
- lumped_storage: float32 [2, 32, 8, 2048], P(None, 'face', 'depth'), may hold values from 1 to 4
- simplex_vertices: int32 [2, 32, 8, 4, 8192], P(None, 'face', 'depth'), may hold values from 0 to 2047
- stiffness_entries: float32 [2, 32, 8, 10, 8192], P(None, 'face', 'depth'), may hold values from -0.3 to 2, as said below
- interface_vertices: int32 [2, 32, 8, 2, 256], P(None, 'face', 'depth'), may hold values from 0 to 2047, as said below
- touching_triangle_vertices: int32 [2, 32, 3, 1024], P(None, 'face'), may hold values from 0 to 2047
- partner_lookup: int32 [32, 1024], replicated, may hold values from 0 to 32767, as said below
- engaged_flags: int32 [32, 1024], P('face'), may hold values 0 or 1
- rotor_gap_quantities: float32 [3, 32, 1024], P(None, 'face'), may hold values from -6 to 6
- lining_orthogonal_motion: float32 [32, 1024], P('face'), may hold values from -6 to 6
- touching_transfer_factor: float32 [32, 1024], P('face'), may hold values from 2 to 16
Outputs:
- advanced_thermal_field: float32 [2, 32, 8, 2048], P(None, 'face', 'depth')
- pressure: float32 [32, 1024], P('face')
Inputs may be any that keep to these rules, and one draw needn't show every extreme that they name: `stiffness_entries`: diagonal entries (the first four components) lie in [1, 2], off-diagonal ones in [-0.3, -0.05]. `interface_vertices`: the two lists of one body on one device name 512 different nodes. Position i of a block's upper list and position i of the lower list of the block above are copies of one node. `partner_lookup`: A disc face may meet a pad face of any patch; several disc faces may meet one pad face.
All inputs are finite; a program needn't handle non-finite values. No bound on the sum of `engaged_flags` on one device may be relied on, other than what follows from the above.
Results may differ from a plain program's by a relative error of at most 0.00002.
Values sent between devices are 32-bit elements; how exact they have to be, the bound alone decides.
No kernel may reach another device: no remote copies, remote signals or barrier semaphores. Data moves between devices by JAX's collectives and lax.ppermute only.
A program may use at most 64 MiB of HBM per device.

v0:
```python
import jax
import jax.numpy as jnp
from jax import lax
from jax.sharding import PartitionSpec as P

increment_factor = 0.05
nitsche = 1.0
film_floor = 0.25


def padded_2(cells, sides, width):
    for axis, dim in sides:
        count = lax.axis_size(axis)
        ends = count - 1
        head = lax.slice_in_dim(cells, 0, width, axis=dim)
        tail = lax.slice_in_dim(cells, cells.shape[dim] - width, cells.shape[dim], axis=dim)
        cells = jnp.concatenate(
            [
                lax.ppermute(tail, axis, [(i, (i + 1) % count) for i in range(ends)]),
                cells,
                lax.ppermute(head, axis, [((i + 1) % count, i) for i in range(ends)]),
            ],
            axis=dim,
        )
    return cells


def element_residual(values, corners, entries):
    picked = values[corners]
    row_one = (
        entries[0] * picked[0]
        + entries[4] * picked[1]
        + entries[5] * picked[2]
        + entries[6] * picked[3]
    )
    row_two = (
        entries[4] * picked[0]
        + entries[1] * picked[1]
        + entries[7] * picked[2]
        + entries[8] * picked[3]
    )
    row_three = (
        entries[5] * picked[0]
        + entries[7] * picked[1]
        + entries[2] * picked[2]
        + entries[9] * picked[3]
    )
    row_four = (
        entries[6] * picked[0]
        + entries[8] * picked[1]
        + entries[9] * picked[2]
        + entries[3] * picked[3]
    )
    stacked = -jnp.stack([row_one, row_two, row_three, row_four])
    return jax.ops.segment_sum(
        stacked.reshape(-1), corners.reshape(-1), num_segments=values.shape[0]
    )


def touching_triangle_values(values, corners):
    picked = values[corners]
    return (picked[0] + picked[1] + picked[2]) / 3.0


def spread_faces(face_rates, corners, solid_vertex_total):
    shares = jnp.broadcast_to(face_rates / 3.0, corners.shape)
    return jax.ops.segment_sum(
        shares.reshape(-1), corners.reshape(-1), num_segments=solid_vertex_total
    )


def set_rims(values, low_at, up_at, low_set, up_set):
    return values.at[low_at].set(low_set).at[up_at].set(up_set)


def local(
    thermal_field,
    lumped_storage,
    simplex_vertices,
    stiffness_entries,
    interface_vertices,
    touching_triangle_vertices,
    partner_lookup,
    engaged_flags,
    rotor_gap_quantities,
    lining_orthogonal_motion,
    touching_transfer_factor,
):
    solid_vertex_total = thermal_field.shape[-1]
    patch_index = lax.axis_index("face")
    depth_index = lax.axis_index("depth")
    surface = (depth_index == 0).astype(jnp.float32)
    thermal_imbalance = jnp.stack(
        [
            element_residual(
                thermal_field[solid_selector, 0, 0],
                simplex_vertices[solid_selector, 0, 0],
                stiffness_entries[solid_selector, 0, 0],
            )
            for solid_selector in range(2)
        ]
    )
    rotor_triangle_values = touching_triangle_values(
        thermal_field[0, 0, 0], touching_triangle_vertices[0, 0]
    )
    lining_triangle_values = touching_triangle_values(
        thermal_field[1, 0, 0], touching_triangle_vertices[1, 0]
    )
    active_mask = engaged_flags[0].astype(jnp.float32)
    displace = rotor_gap_quantities[0, 0]
    opening = rotor_gap_quantities[1, 0]
    multiplier = rotor_gap_quantities[2, 0]
    weight = active_mask * touching_transfer_factor[0]
    own_match = lax.dynamic_slice_in_dim(partner_lookup, patch_index, 1, 0)[0]
    pad_normals, pad_traces = (
        lax.all_gather(lining_orthogonal_motion[0], "face", axis=0, tiled=True),
        lax.all_gather(lining_triangle_values, "face", axis=0, tiled=True),
    )
    pressure = active_mask * jnp.maximum(
        multiplier + nitsche * (displace - pad_normals[own_match] - opening), 0.0
    )
    disc_rate = weight * (film_floor + pressure) * (pad_traces[own_match] - rotor_triangle_values)
    spread = jax.ops.segment_sum(disc_rate, own_match, num_segments=partner_lookup.size)
    pad_rate = -lax.psum_scatter(spread, "face", scatter_dimension=0, tiled=True)
    nodal = jnp.stack(
        [
            spread_faces(disc_rate, touching_triangle_vertices[0, 0], solid_vertex_total),
            spread_faces(pad_rate, touching_triangle_vertices[1, 0], solid_vertex_total),
        ]
    )
    thermal_imbalance = thermal_imbalance + surface * nodal
    lower = interface_vertices[:, 0, 0, 0]
    upper = interface_vertices[:, 0, 0, 1]
    low_values = jnp.take_along_axis(thermal_imbalance, lower, axis=1)
    up_values = jnp.take_along_axis(thermal_imbalance, upper, axis=1)
    rows_both = jnp.stack([low_values.reshape(-1), up_values.reshape(-1)])
    padded = padded_2(rows_both, (("depth", 0),), 1)
    low_new = low_values + padded[0].reshape(low_values.shape)
    up_new = up_values + padded[3].reshape(up_values.shape)
    gathered_imbalance = jax.vmap(set_rims)(thermal_imbalance, lower, upper, low_new, up_new)
    advanced_thermal_field = (
        thermal_field + increment_factor * gathered_imbalance[:, None, None, :] / lumped_storage
    )
    return (advanced_thermal_field, pressure[None])


def solution(mesh):
    placed = (
        P(None, "face", "depth", None),
        P(None, "face", "depth", None),
        P(None, "face", "depth", None, None),
        P(None, "face", "depth", None, None),
        P(None, "face", "depth", None, None),
        P(None, "face", None, None),
        P(),
        P("face", None),
        P(None, "face", None),
        P("face", None),
        P("face", None),
    )
    return jax.shard_map(
        local,
        mesh=mesh,
        in_specs=placed,
        out_specs=(P(None, "face", "depth", None), P("face", None)),
        check_vma=False,
    )
```

profile of v0, /device:TPU:24, one launch (start us, length us, event | category | flops | bytes accessed | tf_op | source)
XLA Modules:
  0.0 958.9 jit_solution(17797581546140559378)
XLA Ops:
  7.2 0.0 all-reduce.3.cloned.1.call-start
  7.2 0.7 fusion.56
  7.9 0.0 copy-start.2
  7.9 0.8 compare_select_fusion.4
  8.7 0.0 copy-done.2
  8.8 17.4 %gather_fusion.3 = f32[3072]{0:T(1024)S(1)} fusion(f32[2048]{0:T(1024)S(1)} %bitcast.281, s32[3072]{0:T(1024)S(1)} %broadcast_clamp_fusion.3), kind=kCustom, calls=%fused_computation.5 | custom fusion | bytes 36864 | tf_op jit(solution)/shard_map/gather | solution.py:61
  26.2 0.0 copy-start.8
  26.2 34.7 %all-gather.1 = f32[1,32768]{1,0:T(1,128)S(1)} all-gather(f32[1,1024]{1,0:T(1,128)S(1)} %bitcast.324), channel_id=3, replica_groups=mesh['face'=32,'depth'=8] {'face'}, dimensions={1}, use_global_device_ids=true | all-gather | bytes 135168 | tf_op jit(solution)/shard_map/all_gather | solution.py:117
  60.9 0.0 copy-done.8
  60.9 34.0 %all-gather = f32[1,32768]{1,0:T(1,128)S(1)} all-gather(f32[1,1024]{1,0:T(1,128)S(1)} %copy-done.8), channel_id=2, replica_groups=mesh['face'=32,'depth'=8] {'face'}, dimensions={1}, use_global_device_ids=true | all-gather | bytes 135168 | tf_op jit(solution)/shard_map/all_gather | solution.py:116
  94.9 6.1 gather_fusion.4
  101.1 6.2 gather_fusion.2
  107.2 0.0 copy-start.4
  107.3 0.7 copy-done.4
  107.9 0.0 copy-start.6
  108.0 0.7 copy-done.6
  108.6 0.0 copy-start.9
  108.6 17.4 %gather_fusion.5 = f32[3072]{0:T(1024)S(1)} fusion(f32[2048]{0:T(1024)S(1)} %bitcast.279, s32[3072]{0:T(1024)S(1)} %broadcast_clamp_fusion.2), kind=kCustom, calls=%fused_computation.7 | custom fusion | bytes 36864 | tf_op jit(solution)/shard_map/gather | solution.py:61
  126.1 0.0 copy-start.1
  126.1 0.0 copy-done.9
  126.1 6.5 scatter_custom_fusion.3
  132.6 0.0 all-reduce.3.cloned.1.call-update
  132.7 0.0 copy-done.1
  132.7 0.1 fusion
  132.8 180.5 %gather_fusion.1 = f32[32768]{0:T(1024)S(1)} fusion(f32[2048]{0:T(1024)S(1)} %bitcast.282, s32[32768]{0:T(1024)S(1)} %broadcast_clamp_fusion), kind=kCustom, calls=%fused_computation.3 | custom fusion | bytes 393216 | tf_op jit(solution)/shard_map/gather | solution.py:29
  313.4 0.0 copy-start
  313.4 180.5 %gather_fusion = f32[32768]{0:T(1024)S(1)} fusion(f32[2048]{0:T(1024)S(1)} %bitcast.280, s32[32768]{0:T(1024)S(1)} %broadcast_clamp_fusion.1), kind=kCustom, calls=%fused_computation.2 | custom fusion | bytes 393216 | tf_op jit(solution)/shard_map/gather | solution.py:29
  494.0 0.0 copy-done
  494.0 0.2 fusion.15
  494.2 0.2 fusion.22
  494.4 0.2 fusion.27
  494.6 0.3 fusion.2
  495.0 0.0 copy-start.5
  495.0 0.7 copy-done.5
  495.7 172.3 %scatter_custom_fusion = f32[2048]{0:T(1024)S(1)} fusion(s32[32768]{0:T(1024)S(1)} %bitcast.308, f32[32768]{0:T(1024)S(1)} %bitcast.307, f32[]{:T(128)} %constant.19.clone.1), kind=kCustom, calls=%fused_computation.121 | custom fusion | flops 32768 | bytes 8196 | tf_op jit(solution)/shard_map/scatter-add | solution.py:55
  668.1 172.3 %scatter_custom_fusion.1 = f32[2048]{0:T(1024)S(1)} fusion(s32[32768]{0:T(1024)S(1)} %bitcast.310, f32[32768]{0:T(1024)S(1)} %bitcast.309, f32[]{:T(128)} %constant.19.clone.1), kind=kCustom, calls=%fused_computation.119 | custom fusion | flops 32768 | bytes 8196 | tf_op jit(solution)/shard_map/scatter-add | solution.py:55
  840.4 0.0 copy-start.10
  840.4 0.7 copy-done.10
  841.1 0.6 dynamic-slice
  842.3 16.7 %scatter_custom_fusion.2 = f32[2048]{0:T(1024)S(1)} fusion(s32[3072]{0:T(1024)S(1)} %bitcast.326, f32[3072]{0:T(1024)S(1)} %reshape.422, f32[]{:T(128)} %constant.19.clone.1), kind=kCustom, calls=%fused_computation.117 | custom fusion | flops 3072 | bytes 8196 | tf_op jit(solution)/shard_map/scatter-add | solution.py:67
  859.0 0.0 all-reduce.3.cloned.1.call-done
  859.0 0.7 fusion.38
  859.7 16.7 %scatter_custom_fusion.4 = f32[2048]{0:T(1024)S(1)} fusion(s32[3072]{0:T(1024)S(1)} %bitcast.325, f32[3072]{0:T(1024)S(1)} %reshape.438, f32[]{:T(128)} %constant.19.clone.1), kind=kCustom, calls=%fused_computation.115 | custom fusion | flops 3072 | bytes 8196 | tf_op jit(solution)/shard_map/scatter-add | solution.py:67
  876.5 4.8 gather_fusion.6
  881.4 5.6 collective-permute-start.1
  886.9 0.6 fusion.37
  887.5 4.8 gather_fusion.7
  892.4 0.0 collective-permute-done.1
  892.4 0.5 broadcast.309
  892.9 0.7 reduce.7
  893.6 1.9 collective-permute-start
  895.6 7.1 collective-permute-done
  902.7 0.7 reduce.6
  903.4 24.0 %scatter_fusion = f32[2,2048]{1,0:T(2,128)S(1)} fusion(f32[2,2048]{1,0:T(2,128)S(1)} %maximum_add_fusion, s32[512]{0:T(512)S(1)} %bitcast.286, f32[512]{0:T(512)S(1)} %bitcast.328), kind=kCustom, calls=%fused_computation.13 | custom fusion | bytes 10240 | tf_op jit(solution)/shard_map/vmap()/scatter | solution.py:73
  927.4 0.0 copy-start.3
  927.4 0.0 copy-start.7
  927.4 24.0 %scatter_fusion.1 = f32[2,2048]{1,0:T(2,128)S(1)} fusion(f32[2,2048]{1,0:T(2,128)S(1)} %scatter_fusion, s32[512]{0:T(512)S(1)} %bitcast.285, f32[512]{0:T(512)S(1)} %bitcast.327), kind=kCustom, calls=%fused_computation.14 | custom fusion | bytes 10240 | tf_op jit(solution)/shard_map/vmap()/scatter | solution.py:73
  951.4 0.0 copy-done.3
  951.4 0.0 copy-done.7
  951.5 0.6 copy.27
  (42 shorter events, 0.5 us)
Async XLA Ops:
  7.2 851.9 %all-reduce.3.cloned.1.call-start = ((), (), s32[]{:S(2)}) async-start(), calls=%async_computation | async-start | bytes 262144
  7.9 0.8 copy-start.2
  26.2 34.7 %copy-start.8 = (f32[1,1024]{1,0:T(1,128)S(1)}, f32[1,1024]{1,0:T(1,128)}, u32[]{:S(2)}) copy-start(f32[1,1024]{1,0:T(1,128)} %param.22) | copy-start | bytes 12292
  107.2 0.7 copy-start.4
  107.9 0.7 copy-start.6
  108.6 17.4 %copy-start.9 = (f32[1,1024]{1,0:T(1,128)S(1)}, f32[1,1024]{1,0:T(1,128)}, u32[]{:S(2)}) copy-start(f32[1,1024]{1,0:T(1,128)} %param.23) | copy-start | bytes 12292
  126.1 6.6 copy-start.1
  313.4 180.6 %copy-start = (f32[2,1,1,10,8192]{4,2,3,1,0:T(1,128)S(1)}, f32[2,1,1,10,8192]{4,2,3,1,0:T(1,128)}, u32[]{:S(2)}) copy-start(f32[2,1,1,10,8192]{4,2,3,1,0:T(1,128)} %param.16) | copy-start | bytes 1966084
  495.0 0.7 copy-start.5
  840.4 0.7 copy-start.10
  881.4 11.0 %collective-permute-start.1 = (f32[1,512]{1,0:T(1,128)S(1)}, f32[1,512]{1,0:T(1,128)S(1)}, u32[]{:S(2)}, u32[]{:S(2)}) collective-permute-start(f32[1,512]{1,0:T(1,128)S(1)} %bitcast.332), channel_id=1, source_target_pairs={{1,0},{2,1},{3,2},{4,3},{5,4},{6,5},{7,6},{9,8},{10,9},{11,10},{12... | collective-permute-start | bytes 6152 | tf_op jit(solution)/shard_map/ppermute | solution.py:21
  893.6 9.1 collective-permute-start
  927.4 24.0 %copy-start.3 = (f32[2,1,1,2048]{3,2,1,0:T(1,128)S(1)}, f32[2,1,1,2048]{3,2,1,0:T(1,128)}, u32[]{:S(2)}) copy-start(f32[2,1,1,2048]{3,2,1,0:T(1,128)} %param.13) | copy-start | bytes 49156
  927.4 24.0 %copy-start.7 = (f32[2,1,1,2048]{3,2,1,0:T(1,128)S(1)}, f32[2,1,1,2048]{3,2,1,0:T(1,128)}, u32[]{:S(2)}) copy-start(f32[2,1,1,2048]{3,2,1,0:T(1,128)} %param.14) | copy-start | bytes 49156
Sparse Core Ops, SparseCore 0:
  132.8 197.5 all-reduce.2
where the time goes:
time: 959 us
  local copies, waits for them, and re-layouts  471 us (49%)
  other arithmetic  389 us (41%)
  blocking collectives  68.7 us (7%)
  between operations  15.2 us (2%)
    gather x2, local copies, waits for them, and re-layouts, element_residual(): picked = values[corners]  361 us
    scatter-add x2, other arithmetic, element_residual(): jax.ops.segment_sum(stacked.reshape(-1), corners.reshape(-1), num_segment...  345 us
    scatter x2, local copies, waits for them, and re-layouts, set_rims(): return values.at[low_at].set(low_set).at[up_at].set(up_set)  47.9 us
    gather x2, local copies, waits for them, and re-layouts, touching_triangle_values(): picked = values[corners]  34.8 us
    all_gather x1, blocking collectives, local(): lax.all_gather(lining_triangle_values, 'face', axis=0, tiled=True)  34.7 us
    all_gather x1, blocking collectives, local(): lax.all_gather(lining_orthogonal_motion[0], 'face', axis=0, tiled=True)  34 us
    scatter-add x2, other arithmetic, spread_faces(): jax.ops.segment_sum(shares.reshape(-1), corners.reshape(-1), num_segments...  33.4 us
  transfers between devices with their start and end apart: 3, of which 1 were waited for; matrix products, arithmetic and copies ran while one was open for 76% of the time, Pallas kernels for 0%

commit v1 on v0

--- a/solution.py
+++ b/solution.py
@@ -114,7 +114,12 @@
     own_match = lax.dynamic_slice_in_dim(partner_lookup, patch_index, 1, 0)[0]
     pad_normals, pad_traces = (
         lax.all_gather(lining_orthogonal_motion[0], "face", axis=0, tiled=True),
-        lax.all_gather(lining_triangle_values, "face", axis=0, tiled=True),
+        jnp.concatenate(
+            lax.all_to_all(
+                jnp.stack([lining_triangle_values] * lax.axis_size("face")), "face", 0, 0
+            ),
+            axis=0,
+        ),
     )
     pressure = active_mask * jnp.maximum(
         multiplier + nitsche * (displace - pad_normals[own_match] - opening), 0.0

time: 959 us -> 1120 us (1.17)
  waiting for transfers between devices: 7.17 us -> 193 us
  blocking collectives: 68.7 us -> 31.3 us
    unnamed x2, waiting for transfers between devices: 0.04 us -> 185 us
    all_gather x1 -> x0, blocking collectives: 34.7 us -> none  [local(): lax.all_gather(lining_triangle_values, 'face', axis=0, tiled=True)]
  transfers between devices with their start and end apart: 3 -> 4, of which waited for: 1 -> 2; matrix products, arithmetic and copies ran while one was open for 76% -> 67% of each run, Pallas kernels for 0% -> 0%
where the time goes in v1:
time: 1120 us
  local copies, waits for them, and re-layouts  472 us (42%)
  other arithmetic  389 us (35%)
  waiting for transfers between devices  193 us (17%)
  blocking collectives  31.3 us (3%)
  starting transfers between devices  17.2 us (2%)
  between operations  15.2 us (1%)
    gather x2, local copies, waits for them, and re-layouts, element_residual(): picked = values[corners]  361 us
    scatter-add x2, other arithmetic, element_residual(): jax.ops.segment_sum(stacked.reshape(-1), corners.reshape(-1), num_segment...  345 us
    unnamed x2, waiting for transfers between devices  185 us
    scatter x2, local copies, waits for them, and re-layouts, set_rims(): return values.at[low_at].set(low_set).at[up_at].set(up_set)  47.9 us
    gather x2, local copies, waits for them, and re-layouts, touching_triangle_values(): picked = values[corners]  34.8 us
    scatter-add x2, other arithmetic, spread_faces(): jax.ops.segment_sum(shares.reshape(-1), corners.reshape(-1), num_segments...  33.4 us
    all_gather x1, blocking collectives, local(): lax.all_gather(lining_orthogonal_motion[0], 'face', axis=0, tiled=True)  31.3 us
  transfers between devices with their start and end apart: 4, of which 2 were waited for; matrix products, arithmetic and copies ran while one was open for 67% of the time, Pallas kernels for 0%

profile of v1, /device:TPU:24, one launch (start us, length us, event | category | flops | bytes accessed | tf_op | source)
XLA Modules:
  0.0 1117.2 jit_solution(14202721247319395673)
XLA Ops:
  7.2 0.0 copy-start.2
  7.2 0.7 fusion.56
  7.9 0.0 copy-done.2
  7.9 17.4 %gather_fusion.3 = f32[3072]{0:T(1024)S(1)} fusion(f32[2048]{0:T(1024)S(1)} %bitcast.280, s32[3072]{0:T(1024)S(1)} %broadcast_clamp_fusion.3), kind=kCustom, calls=%fused_computation.5 | custom fusion | bytes 36864 | tf_op jit(solution)/shard_map/gather | solution.py:61
  25.4 0.0 copy-start.1
  25.4 0.7 stack.23
  26.1 10.1 all-to-all-start
  36.2 0.0 all-reduce.3.cloned.1.call-start
  36.2 0.0 copy-done.1
  36.3 0.1 fusion
  36.4 180.5 %gather_fusion.1 = f32[32768]{0:T(1024)S(1)} fusion(f32[2048]{0:T(1024)S(1)} %bitcast.281, s32[32768]{0:T(1024)S(1)} %broadcast_clamp_fusion), kind=kCustom, calls=%fused_computation.3 | custom fusion | bytes 393216 | tf_op jit(solution)/shard_map/gather | solution.py:29
  217.0 0.0 copy-start
  217.0 180.5 %gather_fusion = f32[32768]{0:T(1024)S(1)} fusion(f32[2048]{0:T(1024)S(1)} %bitcast.278, s32[32768]{0:T(1024)S(1)} %broadcast_clamp_fusion.1), kind=kCustom, calls=%fused_computation.2 | custom fusion | bytes 393216 | tf_op jit(solution)/shard_map/gather | solution.py:29
  397.6 0.0 copy-done
  397.6 0.2 fusion.15
  397.8 0.2 fusion.22
  398.0 0.2 fusion.27
  398.2 0.8 compare_select_fusion.4
  399.0 0.0 copy-start.5
  399.0 0.7 copy-done.5
  399.7 0.0 copy-start.8
  399.7 0.3 fusion.2
  400.0 0.4 copy-done.8
  400.4 31.3 %all-gather = f32[1,32768]{1,0:T(1,128)S(1)} all-gather(f32[1,1024]{1,0:T(1,128)S(1)} %copy-done.8), channel_id=2, replica_groups=mesh['face'=32,'depth'=8] {'face'}, dimensions={1}, use_global_device_ids=true | all-gather | bytes 135168 | tf_op jit(solution)/shard_map/all_gather | solution.py:116
  431.8 0.0 copy-start.6
  431.8 17.4 %gather_fusion.5 = f32[3072]{0:T(1024)S(1)} fusion(f32[2048]{0:T(1024)S(1)} %bitcast.279, s32[3072]{0:T(1024)S(1)} %broadcast_clamp_fusion.2), kind=kCustom, calls=%fused_computation.7 | custom fusion | bytes 36864 | tf_op jit(solution)/shard_map/gather | solution.py:61
  449.2 0.0 copy-done.6
  449.3 172.3 %scatter_custom_fusion = f32[2048]{0:T(1024)S(1)} fusion(s32[32768]{0:T(1024)S(1)} %bitcast.307, f32[32768]{0:T(1024)S(1)} %bitcast.306, f32[]{:T(128)} %constant.19.clone.1), kind=kCustom, calls=%fused_computation.121 | custom fusion | flops 32768 | bytes 8196 | tf_op jit(solution)/shard_map/scatter-add | solution.py:55
  621.6 172.3 %scatter_custom_fusion.1 = f32[2048]{0:T(1024)S(1)} fusion(s32[32768]{0:T(1024)S(1)} %bitcast.309, f32[32768]{0:T(1024)S(1)} %bitcast.308, f32[]{:T(128)} %constant.19.clone.1), kind=kCustom, calls=%fused_computation.119 | custom fusion | flops 32768 | bytes 8196 | tf_op jit(solution)/shard_map/scatter-add | solution.py:55
  793.9 6.2 gather_fusion.2
  800.1 0.0 copy-start.4
  800.1 0.0 copy-start.10
  800.1 0.7 copy-done.10
  800.8 0.6 dynamic-slice
  802.0 0.0 copy-done.4
  802.0 0.0 all-to-all-done
  802.0 6.2 gather_fusion.4
  808.2 0.0 copy-start.9
  808.2 0.7 copy-done.9
  808.9 6.5 scatter_custom_fusion.3
  815.5 0.0 all-reduce.3.cloned.1.call-update
  815.5 16.7 %scatter_custom_fusion.2 = f32[2048]{0:T(1024)S(1)} fusion(s32[3072]{0:T(1024)S(1)} %bitcast.324, f32[3072]{0:T(1024)S(1)} %reshape.430, f32[]{:T(128)} %constant.19.clone.1), kind=kCustom, calls=%fused_computation.117 | custom fusion | flops 3072 | bytes 8196 | tf_op jit(solution)/shard_map/scatter-add | solution.py:67
  832.2 185.5 %all-reduce.3.cloned.1.call-done = f32[32768]{0:T(1024)} async-done(((f32[32768]{0:T(1024)}), f32[32768]{0:T(1024)}) %all-reduce.3.cloned.1.call-update) | async-done | bytes 131088
  1017.7 0.7 fusion.38
  1018.4 16.7 %scatter_custom_fusion.4 = f32[2048]{0:T(1024)S(1)} fusion(s32[3072]{0:T(1024)S(1)} %bitcast.323, f32[3072]{0:T(1024)S(1)} %reshape.446, f32[]{:T(128)} %constant.19.clone.1), kind=kCustom, calls=%fused_computation.115 | custom fusion | flops 3072 | bytes 8196 | tf_op jit(solution)/shard_map/scatter-add | solution.py:67
  1035.1 4.8 gather_fusion.6
  1040.0 5.2 collective-permute-start.1
  1045.2 0.6 fusion.37
  1045.8 4.8 gather_fusion.7
  1050.6 0.0 collective-permute-done.1
  1050.7 0.5 broadcast.315
  1051.2 0.7 reduce.7
  1051.9 1.9 collective-permute-start
  1053.8 7.1 collective-permute-done
  1061.0 0.7 reduce.6
  1061.7 24.0 %scatter_fusion = f32[2,2048]{1,0:T(2,128)S(1)} fusion(f32[2,2048]{1,0:T(2,128)S(1)} %maximum_add_fusion, s32[512]{0:T(512)S(1)} %bitcast.285, f32[512]{0:T(512)S(1)} %bitcast.326), kind=kCustom, calls=%fused_computation.13 | custom fusion | bytes 10240 | tf_op jit(solution)/shard_map/vmap()/scatter | solution.py:73
  1085.6 0.0 copy-start.3
  1085.6 0.0 copy-start.7
  1085.6 24.0 %scatter_fusion.1 = f32[2,2048]{1,0:T(2,128)S(1)} fusion(f32[2,2048]{1,0:T(2,128)S(1)} %scatter_fusion, s32[512]{0:T(512)S(1)} %bitcast.284, f32[512]{0:T(512)S(1)} %bitcast.325), kind=kCustom, calls=%fused_computation.14 | custom fusion | bytes 10240 | tf_op jit(solution)/shard_map/vmap()/scatter | solution.py:73
  1109.6 0.0 copy-done.3
  1109.7 0.0 copy-done.7
  1109.7 0.6 copy.27
  (42 shorter events, 0.5 us)
Async XLA Ops:
  7.2 0.7 copy-start.2
  25.4 10.9 copy-start.1
  26.1 775.9 %all-to-all-start = ((f32[32,1,1024]{2,1,0:T(1,128)}), f32[32,1,1024]{2,1,0:T(1,128)S(1)}, u32[]{:S(2)}, u32[]{:S(2)}) async-start(f32[32,1,1024]{2,1,0:T(1,128)} %stack.23), calls=%async_computation | async-start | bytes 262144 | tf_op jit(solution)/shard_map/all_to_all | solution.py:118
  36.2 981.5 %all-reduce.3.cloned.1.call-start = ((), (), s32[]{:S(2)}) async-start(), calls=%async_computation.1 | async-start | bytes 262144
  217.0 180.6 %copy-start = (f32[2,1,1,10,8192]{4,2,3,1,0:T(1,128)S(1)}, f32[2,1,1,10,8192]{4,2,3,1,0:T(1,128)}, u32[]{:S(2)}) copy-start(f32[2,1,1,10,8192]{4,2,3,1,0:T(1,128)} %param.16) | copy-start | bytes 1966084
  399.0 0.7 copy-start.5
  399.7 0.7 copy-start.8
  431.8 17.4 %copy-start.6 = (s32[1,1024]{1,0:T(1,128)S(1)}, s32[1,1024]{1,0:T(1,128)}, u32[]{:S(2)}) copy-start(s32[1,1024]{1,0:T(1,128)} %param.20) | copy-start | bytes 12292
  800.1 1.9 copy-start.4
  800.1 0.7 copy-start.10
  808.2 0.7 copy-start.9
  1040.0 10.6 collective-permute-start.1
  1051.9 9.1 collective-permute-start
  1085.6 24.0 %copy-start.3 = (f32[2,1,1,2048]{3,2,1,0:T(1,128)S(1)}, f32[2,1,1,2048]{3,2,1,0:T(1,128)}, u32[]{:S(2)}) copy-start(f32[2,1,1,2048]{3,2,1,0:T(1,128)} %param.13) | copy-start | bytes 49156
  1085.6 24.0 %copy-start.7 = (f32[2,1,1,2048]{3,2,1,0:T(1,128)S(1)}, f32[2,1,1,2048]{3,2,1,0:T(1,128)}, u32[]{:S(2)}) copy-start(f32[2,1,1,2048]{3,2,1,0:T(1,128)} %param.14) | copy-start | bytes 49156
Sparse Core Ops, SparseCore 0:
  815.6 202.0 all-reduce.2
